TPU v7x, 128 devices: a whole 4x4x4 slice. The times are simulated.
128 devices in a mesh: gx: 16 (over x, y), gy: 8 (over z, core).
Axes of the slice: x: 4, y: 4, z: 4, core: 2. Of those that a mesh axis runs over, the one named last changes fastest.
Arguments:
- field: float32 [256, 256, 1536], P('gx', 'gy'), may hold values from -24 to 24
- kappa: float32 [256, 256, 1536], P('gx', 'gy'), may hold values from 0.02 to 0.16
- history: float32 [126, 128, 64, 128], P(None, 'gx', 'gy'), may hold values from -2400 to 2400
Outputs:
- field_next: float32 [256, 256, 1536], P('gx', 'gy')
- basis: float32 [128, 128, 64, 128], P(None, 'gx', 'gy')
- factor: float32 [128, 128], replicated
All inputs are finite; a program needn't handle non-finite values.
Results may differ from a plain program's by a relative error of at most 0.00018.
Values sent between devices are 32-bit elements; how exact they have to be, the bound alone decides.
No kernel may reach another device: no remote copies, remote signals or barrier semaphores. Data moves between devices by JAX's collectives and lax.ppermute only.
A program may use at most 192 MiB of HBM per device.

v0:
```python
import jax
import jax.numpy as jnp
from jax import lax
from jax.sharding import PartitionSpec as P


def extended(block, sides, width):
    for axis, dim in sides:
        count = lax.axis_size(axis)
        forward = [(i, i + 1) for i in range(count - 1)]
        backward = [(target, source) for source, target in forward]
        low = lax.ppermute(
            lax.slice_in_dim(block, block.shape[dim] - width, None, axis=dim), axis, forward
        )
        high = lax.ppermute(lax.slice_in_dim(block, 0, width, axis=dim), axis, backward)
        block = jnp.concatenate([low, block, high], axis=dim)
    return block


def advance(field_pad, kappa_pad):
    field_z = jnp.pad(field_pad, ((0, 0), (0, 0), (1, 1)))
    kappa_z = jnp.pad(kappa_pad, ((0, 0), (0, 0), (1, 1)))
    centre = field_z[1:-1, 1:-1, 1:-1]
    kcentre = kappa_z[1:-1, 1:-1, 1:-1]
    places = [
        (slice(2, None), slice(1, -1), slice(1, -1)),
        (slice(None, -2), slice(1, -1), slice(1, -1)),
        (slice(1, -1), slice(2, None), slice(1, -1)),
        (slice(1, -1), slice(None, -2), slice(1, -1)),
        (slice(1, -1), slice(1, -1), slice(2, None)),
        (slice(1, -1), slice(1, -1), slice(None, -2)),
    ]
    change = jnp.zeros_like(centre)
    for place in places:
        change = change + 0.5 * (kcentre + kappa_z[place]) * (field_z[place] - centre)
    return centre + change


def sample(field):
    a, b, c = field.shape
    return field.reshape(a // 2, 2, b // 4, 4, c // 12, 12)[:, 0, :, 0, :, 0]


def body(field, kappa, history):
    both = jnp.stack([field, kappa])
    padded = extended(both, (("gx", 1), ("gy", 2)), 1)
    kappa_pad = padded[1]
    first = advance(padded[0], kappa_pad)
    first_pad = extended(first, (("gx", 0), ("gy", 1)), 1)
    second = advance(first_pad, kappa_pad)
    block = jnp.concatenate([history, sample(first)[None], sample(second)[None]], 0)
    shape = block.shape
    block = block.reshape(shape[0], -1)
    rows_all = block.shape[1] * lax.axis_size("gx") * lax.axis_size("gy")
    gram = jnp.einsum("ar,br->ab", block, block, precision=lax.Precision.HIGHEST) / rows_all
    total = lax.psum(gram, ("gx", "gy"))
    factor = jnp.linalg.cholesky(total).T
    basis = lax.linalg.triangular_solve(factor.T, block, left_side=True, lower=True)
    return (second, basis.reshape(shape), factor)


def solution(mesh):
    placed = (P("gx", "gy", None), P("gx", "gy", None), P(None, "gx", "gy", None))
    return jax.shard_map(
        body,
        mesh=mesh,
        in_specs=placed,
        out_specs=(P("gx", "gy", None), P(None, "gx", "gy", None), P()),
        check_vma=False,
    )
```

profile of v0, /device:TPU:1, one launch (start us, length us, event | category | flops | bytes accessed | tf_op | source)
XLA Modules:
  0.0 410.7 jit_solution(8603581438563554559)
XLA Ops:
  7.2 1.4 pad_maximum_fusion.11
  8.7 4.2 %collective-permute-start = (f32[2,1,32,1536]{3,2,1,0:T(8,128)S(1)}, f32[2,1,32,1536]{3,2,1,0:T(8,128)S(1)}, u32[]{:S(2)}, u32[]{:S(2)}) collective-permute-start(f32[2,1,32,1536]{3,2,1,0:T(8,128)S(1)} %get-tuple-element.19), channel_id=1, source_target_pairs={{0,8},{8,16},{16,24},{24,32},{32,40},{40,48},{48,56},{56,64},{64,7... | collective-permute-start | bytes 1179656 | tf_op jit(solution)/shard_map/ppermute | solution.py:12
  12.8 1.3 collective-permute-start.1
  14.1 6.5 %collective-permute-done = f32[2,1,32,1536]{3,2,1,0:T(8,128)S(1)} collective-permute-done((f32[2,1,32,1536]{3,2,1,0:T(8,128)S(1)}, f32[2,1,32,1536]{3,2,1,0:T(8,128)S(1)}, u32[]{:S(2)}, u32[]{:S(2)}) %collective-permute-start) | collective-permute-done | bytes 393248 | tf_op jit(solution)/shard_map/ppermute | solution.py:12
  20.6 3.9 collective-permute-done.1
  24.5 0.3 pad_maximum_fusion.15
  24.8 5.2 %collective-permute-start.2 = (f32[2,18,1,1536]{3,2,1,0:T(1,128)S(1)}, f32[2,18,1,1536]{3,2,1,0:T(1,128)S(1)}, u32[]{:S(2)}, u32[]{:S(2)}) collective-permute-start(f32[2,18,1,1536]{3,2,1,0:T(1,128)S(1)} %get-tuple-element.17), channel_id=1, source_target_pairs={{0,1},{1,2},{2,3},{3,4},{4,5},{5,6},{6,7},{8,9},{9,10},{10,11},{11... | collective-permute-start | bytes 663560 | tf_op jit(solution)/shard_map/ppermute | solution.py:12
  30.1 1.9 collective-permute-start.3
  32.0 0.9 collective-permute-done.2
  32.9 4.4 %collective-permute-done.3 = f32[2,18,1,1536]{3,2,1,0:T(1,128)S(1)} collective-permute-done((f32[2,18,1,1536]{3,2,1,0:T(1,128)S(1)}, f32[2,18,1,1536]{3,2,1,0:T(1,128)S(1)}, u32[]{:S(2)}, u32[]{:S(2)}) %collective-permute-start.3) | collective-permute-done | bytes 221216 | tf_op jit(solution)/shard_map/ppermute | solution.py:15
  37.3 1.7 pad_maximum_fusion
  39.0 4.2 %slice_bitcast_fusion = (f32[18,34,1536]{2,1,0:T(8,128)}, f32[18,34,1536]{2,1,0:T(8,128)}) fusion(f32[2,18,34,1536]{3,2,1,0:T(8,128)S(1)} %pad_maximum_fusion), kind=kLoop, calls=%fused_computation.12 | loop fusion | bytes 15040512 | tf_op jit(solution)/shard_map/squeeze | solution.py:47
  43.2 28.3 %fusion.15 = f32[16,32,1536]{2,1,0:T(8,128)S(1)} fusion(f32[18,34,1536]{2,1,0:T(8,128)} %get-tuple-element.16, f32[18,34,1536]{2,1,0:T(8,128)} %get-tuple-element.15), kind=kLoop, calls=%fused_computation.29 | loop fusion | flops 23592960 | bytes 43450368 | tf_op jit(solution)/shard_map/add | solution.py:36
  71.6 1.6 collective-permute-start.4
  73.1 4.0 collective-permute-start.5
  77.1 1.1 collective-permute-done.4
  78.2 1.5 collective-permute-done.5
  79.7 0.2 pad_maximum_fusion.16
  79.9 0.7 copy.42
  80.6 1.9 collective-permute-start.6
  82.5 0.7 copy.44
  83.1 4.0 collective-permute-start.7
  87.2 4.3 %copy.50 = f32[126,8,8,128]{3,0,2,1:T(8,128)} copy(f32[126,8,8,128]{3,2,1,0:T(8,128)S(1)} %copy-done.2) | data formatting | bytes 8257536 | tf_op args[2]
  91.5 5.9 %copy.63 = f32[126,8,8,128]{0,3,2,1:T(8,128)} copy(f32[126,8,8,128]{3,2,1,0:T(8,128)} %param.5) | data formatting | bytes 8257536 | tf_op jit(solution)/shard_map/concatenate | solution.py:51
  97.5 38.1 %reshape.29 = f32[8,2,8,4,128,12]{5,4,3,2,1,0:T(8,128)} reshape(f32[16,32,1536]{2,1,0:T(8,128)S(1)} %fusion.15) | data formatting | bytes 6291456 | tf_op jit(solution)/shard_map/reshape | solution.py:41
  135.6 4.7 %slice.184 = f32[8,1,8,1,128,1]{5,4,3,2,1,0:T(8,128)} slice(f32[8,2,8,4,128,12]{5,4,3,2,1,0:T(8,128)} %reshape.29), slice={[0:8], [0:1], [0:8], [0:1], [0:128], [0:1]} | slice | bytes 65536 | tf_op jit(solution)/shard_map/slice | solution.py:41
  140.3 3.4 copy.64
  143.8 3.3 copy.54
  147.1 1.0 copy.43
  148.1 1.2 copy.45
  149.3 4.7 %select_maximum_fusion = f32[18,34,1538]{2,1,0:T(8,128)S(1)} fusion(f32[18,1,1536]{2,1,0:T(1,128)S(1)} %copy.43, f32[18,1,1536]{2,1,0:T(1,128)S(1)} %copy.45, f32[1,32,1536]{2,1,0:T(8,128)S(1)} %collective-permute-done.4, f32[16,32,1536]{2,1,0:T(8,128)S(1)} %fusion.15, f32[1,32,1536]{2,1,0:T(8,128)S(1)} %collective-permute-done.5), kind=kLoop, calls=%fused_computation.3 | loop fusion | flops 11295072 | bytes 7525152 | tf_op jit(solution)/shard_map/concatenate | solution.py:16
  154.0 12.9 %fusion.20 = f32[16,32,1536]{2,1,0:T(8,128)} fusion(f32[16,32,1536]{2,1,0:T(8,128)S(1)} %fusion.15, f32[18,34,1538]{2,1,0:T(8,128)S(1)} %select_maximum_fusion, f32[18,1,1536]{2,1,0:T(1,128)S(1)} %copy.45, f32[1,32,1536]{2,1,0:T(8,128)S(1)} %collective-permute-done.4, f32[1,32,1536]{2,1,0:T(8,128)S(1)} %collective-permute-done.5, ...), kind=kLoop, calls=%fused_computation.35 | loop fusion | flops 29884416 | bytes 33349632 | tf_op jit(solution)/shard_map/add | solution.py:36
  167.0 39.1 %reshape.30 = f32[8,2,8,4,128,12]{5,4,3,2,1,0:T(8,128)} reshape(f32[16,32,1536]{2,1,0:T(8,128)} %fusion.20) | data formatting | bytes 6291456 | tf_op jit(solution)/shard_map/reshape | solution.py:41
  206.1 4.7 %slice.185 = f32[8,1,8,1,128,1]{5,4,3,2,1,0:T(8,128)} slice(f32[8,2,8,4,128,12]{5,4,3,2,1,0:T(8,128)} %reshape.30), slice={[0:8], [0:1], [0:8], [0:1], [0:128], [0:1]} | slice | bytes 65536 | tf_op jit(solution)/shard_map/slice | solution.py:41
  210.8 2.8 copy.65
  213.7 7.7 %fusion.48 = f32[128,128]{0,1:T(8,128)} fusion(f32[1,8,8,128]{3,0,2,1:T(1,128)S(1)} %bitcast.44, f32[1,8,8,128]{3,0,2,1:T(1,128)S(1)} %bitcast.43, f32[126,8,8,128]{3,0,2,1:T(8,128)} %copy.50), kind=kOutput, calls=%fused_computation.78 | convolution fusion | flops 1612726272 | bytes 4259840 | tf_op jit(solution)/shard_map/ar,br->ab/dot_general | solution.py:55
  221.4 2.8 copy.55
  224.2 8.9 %pad_maximum_fusion.1 = f32[128,8192]{0,1:T(8,128)} fusion(f32[1,8192]{0,1:T(8,128)} %copy.55, f32[1,8192]{0,1:T(8,128)} %copy.54, f32[126,8192]{0,1:T(8,128)} %bitcast.40), kind=kLoop, calls=%fused_computation.20 | loop fusion | flops 2097152 | bytes 8388608 | tf_op jit(solution)/shard_map/concatenate | solution.py:51
  233.1 135.0 %all-reduce.5.cloned.1.call-done = f32[128,128]{0,1:T(8,128)} async-done(((f32[128,128]{0,1:T(8,128)}), f32[128,128]{0,1:T(8,128)}) %all-reduce.5.cloned.1.call-update) | async-done | bytes 65552 | tf_op jit(solution)/shard_map/psum | solution.py:56
  368.1 0.9 copy.52
  369.0 0.9 fusion.53
  369.9 11.7 %cholesky.16 = f32[128,128]{1,0:T(8,128)S(1)} custom-call(f32[128,128]{1,0:T(8,128)S(1)} %fusion.53), custom_call_target="Cholesky" | custom-call | tf_op jit(solution)/shard_map/jit(cholesky)/cholesky | solution.py:57
  381.6 0.6 compare_reduce_fusion
  382.3 0.7 fusion.54
  382.9 9.8 %custom-call.6 = f32[1,128,128]{1,2,0:T(8,128)S(1)} custom-call(f32[1,128,128]{2,1,0:T(8,128)S(1)} %get-tuple-element.26), custom_call_target="InvertDiagBlocksLowerTriangular" | custom-call | tf_op jit(solution)/shard_map/triangular_solve | solution.py:58
  392.7 5.7 %fusion.51 = f32[128,8,8,128]{3,0,2,1:T(8,128)S(1)} fusion(f32[8,8,128,128]{3,2,1,0:T(8,128)} %bitcast.41, f32[1,128,128]{1,2,0:T(8,128)S(1)} %custom-call.6), kind=kOutput, calls=%fused_computation.88 | convolution fusion | flops 1610612736 | bytes 8454144 | tf_op jit(solution)/shard_map/triangular_solve | solution.py:58
  398.4 4.4 %copy.57 = f32[128,8,8,128]{3,2,1,0:T(8,128)} copy(f32[128,8,8,128]{3,0,2,1:T(8,128)S(1)} %fusion.51) | data formatting | bytes 8388608
  402.9 0.7 copy.58
  (19 shorter events, 0.2 us)
Async XLA Ops:
  7.2 360.9 %all-reduce.5.cloned.1.call-start = ((), (), s32[]{:S(2)}) async-start(), calls=%async_computation | async-start | bytes 131072 | tf_op jit(solution)/shard_map/psum | solution.py:56
  7.2 17.2 %copy-start = (f32[16,32,1536]{2,1,0:T(8,128)S(1)}, f32[16,32,1536]{2,1,0:T(8,128)}, u32[]{:S(2)}) copy-start(f32[16,32,1536]{2,1,0:T(8,128)} %param.4) | copy-start | bytes 9437188
  7.2 17.2 %copy-start.1 = (f32[16,32,1536]{2,1,0:T(8,128)S(1)}, f32[16,32,1536]{2,1,0:T(8,128)}, u32[]{:S(2)}) copy-start(f32[16,32,1536]{2,1,0:T(8,128)} %param.3) | copy-start | bytes 9437188
  8.7 11.9 %collective-permute-start = (f32[2,1,32,1536]{3,2,1,0:T(8,128)S(1)}, f32[2,1,32,1536]{3,2,1,0:T(8,128)S(1)}, u32[]{:S(2)}, u32[]{:S(2)}) collective-permute-start(f32[2,1,32,1536]{3,2,1,0:T(8,128)S(1)} %get-tuple-element.19), channel_id=1, source_target_pairs={{0,8},{8,16},{16,24},{24,32},{32,40},{40,48},{48,56},{56,64},{64,7... | collective-permute-start | bytes 1179656 | tf_op jit(solution)/shard_map/ppermute | solution.py:12
  12.8 11.6 %collective-permute-start.1 = (f32[2,1,32,1536]{3,2,1,0:T(8,128)S(1)}, f32[2,1,32,1536]{3,2,1,0:T(8,128)S(1)}, u32[]{:S(2)}, u32[]{:S(2)}) collective-permute-start(f32[2,1,32,1536]{3,2,1,0:T(8,128)S(1)} %get-tuple-element.20), channel_id=1, source_target_pairs={{8,0},{16,8},{24,16},{32,24},{40,32},{48,40},{56,48},{64,56},{72,6... | collective-permute-start | bytes 1179656 | tf_op jit(solution)/shard_map/ppermute | solution.py:15
  24.8 8.1 %collective-permute-start.2 = (f32[2,18,1,1536]{3,2,1,0:T(1,128)S(1)}, f32[2,18,1,1536]{3,2,1,0:T(1,128)S(1)}, u32[]{:S(2)}, u32[]{:S(2)}) collective-permute-start(f32[2,18,1,1536]{3,2,1,0:T(1,128)S(1)} %get-tuple-element.17), channel_id=1, source_target_pairs={{0,1},{1,2},{2,3},{3,4},{4,5},{5,6},{6,7},{8,9},{9,10},{10,11},{11... | collective-permute-start | bytes 663560 | tf_op jit(solution)/shard_map/ppermute | solution.py:12
  30.1 7.3 %collective-permute-start.3 = (f32[2,18,1,1536]{3,2,1,0:T(1,128)S(1)}, f32[2,18,1,1536]{3,2,1,0:T(1,128)S(1)}, u32[]{:S(2)}, u32[]{:S(2)}) collective-permute-start(f32[2,18,1,1536]{3,2,1,0:T(1,128)S(1)} %get-tuple-element.18), channel_id=1, source_target_pairs={{1,0},{2,1},{3,2},{4,3},{5,4},{6,5},{7,6},{9,8},{10,9},{11,10},{12... | collective-permute-start | bytes 663560 | tf_op jit(solution)/shard_map/ppermute | solution.py:15
  71.5 15.7 %copy-start.2 = (f32[126,8,8,128]{3,2,1,0:T(8,128)S(1)}, f32[126,8,8,128]{3,2,1,0:T(8,128)}, u32[]{:S(2)}) copy-start(f32[126,8,8,128]{3,2,1,0:T(8,128)} %param.5) | copy-start | bytes 12386308
  71.6 6.7 %collective-permute-start.4 = (f32[1,32,1536]{2,1,0:T(8,128)S(1)}, f32[1,32,1536]{2,1,0:T(8,128)S(1)}, u32[]{:S(2)}, u32[]{:S(2)}) collective-permute-start(f32[1,32,1536]{2,1,0:T(8,128)S(1)} %get-tuple-element.24), channel_id=1, source_target_pairs={{8,0},{16,8},{24,16},{32,24},{40,32},{48,40},{56,48},{64,56},{72,6... | collective-permute-start | bytes 589832 | tf_op jit(solution)/shard_map/ppermute | solution.py:15
  73.1 6.6 %collective-permute-start.5 = (f32[1,32,1536]{2,1,0:T(8,128)S(1)}, f32[1,32,1536]{2,1,0:T(8,128)S(1)}, u32[]{:S(2)}, u32[]{:S(2)}) collective-permute-start(f32[1,32,1536]{2,1,0:T(8,128)S(1)} %get-tuple-element.23), channel_id=1, source_target_pairs={{0,8},{8,16},{16,24},{24,32},{32,40},{40,48},{48,56},{56,64},{64,7... | collective-permute-start | bytes 589832 | tf_op jit(solution)/shard_map/ppermute | solution.py:12
  80.6 66.5 %collective-permute-start.6 = (f32[18,1,1536]{2,0,1:T(8,128)}, f32[18,1,1536]{2,0,1:T(8,128)}, u32[]{:S(2)}, u32[]{:S(2)}) collective-permute-start(f32[18,1,1536]{2,0,1:T(8,128)} %copy.42), channel_id=1, source_target_pairs={{1,0},{2,1},{3,2},{4,3},{5,4},{6,5},{7,6},{9,8},{10,9},{11,10},{12... | collective-permute-start | bytes 331784 | tf_op jit(solution)/shard_map/ppermute | solution.py:15
  83.1 65.0 %collective-permute-start.7 = (f32[18,1,1536]{2,0,1:T(8,128)}, f32[18,1,1536]{2,0,1:T(8,128)}, u32[]{:S(2)}, u32[]{:S(2)}) collective-permute-start(f32[18,1,1536]{2,0,1:T(8,128)} %copy.44), channel_id=1, source_target_pairs={{0,1},{1,2},{2,3},{3,4},{4,5},{5,6},{6,7},{8,9},{9,10},{10,11},{11... | collective-permute-start | bytes 331784 | tf_op jit(solution)/shard_map/ppermute | solution.py:12
  148.1 5.9 %slice-start = ((s8[4423680]{0:T(1024)(128)(4,1)}), s8[4194304]{0:T(1024)(128)(4,1)S(1)}, s32[]{:S(2)}) async-start(s8[4423680]{0:T(1024)(128)(4,1)} %bitcast.32), calls=%async_computation.1 | async-start | bytes 8388608
  149.3 4.7 %slice-start.1 = ((s8[4423680]{0:T(1024)(128)(4,1)}), s8[229376]{0:T(1024)(128)(4,1)S(1)}, s32[]{:S(2)}) async-start(s8[4423680]{0:T(1024)(128)(4,1)} %bitcast.32), calls=%async_computation.2 | async-start | bytes 458752
  210.8 2.8 copy-start.3
Sparse Core Ops, SparseCore 0:
  221.5 146.5 all-reduce.4
where the time goes:
time: 419 us; the launch traced here: 411 us
  waiting for transfers between devices  153 us (37%)
  local copies, waits for them, and re-layouts  123 us (29%)
  other arithmetic  82.1 us (20%)
  starting transfers between devices  24.2 us (6%)
  between operations  14.5 us (3%)
  matrix products  13.4 us (3%)
    psum x1, waiting for transfers between devices, body(): total = lax.psum(gram, ('gx', 'gy'))  135 us
    reshape x2, local copies, waits for them, and re-layouts, sample(): return field.reshape(a // 2, 2, b // 4, 4, c // 12, 12)[:, 0, :, 0, :, 0]  77.3 us
    add x2, other arithmetic, advance(): return centre + change  41.3 us
    ppermute x4, starting transfers between devices, extended(): lax.ppermute(lax.slice_in_dim(block, block.shape[dim] - width, None, axis...  17.4 us
    unnamed x17, local copies, waits for them, and re-layouts  15.8 us
    another operation x3, other arithmetic, body(): factor = jnp.linalg.cholesky(total).T  12.4 us
    concatenate x3, local copies, waits for them, and re-layouts, body(): jnp.concatenate([history, sample(first)[None], sample(second)[None]], 0)  12.1 us
    another operation x1, other arithmetic, body(): lax.linalg.triangular_solve(factor.T, block, left_side=True, lower=True)  9.81 us
  transfers between devices with their start and end apart: 9, of which 7 were waited for; matrix products, arithmetic and copies ran while one was open for 18% of the time, Pallas kernels for 0%

commit v1 on v0

v1 whole, which is shorter than its diff:
```python
import functools

import jax
import jax.numpy as jnp
from jax import lax
from jax.experimental import pallas as pl
from jax.experimental.pallas import tpu as pltpu
from jax.sharding import PartitionSpec as P

F32, BF16 = jnp.float32, jnp.bfloat16
NT = (((1,), (1,)), ((), ()))

def split(x):
    hi = x.astype(BF16)
    return hi, (x - hi.astype(F32)).astype(BF16)

def gram_kernel(h_ref, g_ref, acc):
    i = pl.program_id(0)
    past = h_ref.shape[0]
    flat = h_ref.reshape(past * 8, 128)
    pad = jnp.zeros((128 - past, 128), F32)
    his, los = [], []
    for j in range(8):
        m = jnp.concatenate([flat[pl.ds(j, past, stride=8), :], pad], axis=0)
        hi, lo = split(m)
        his.append(hi); los.append(lo)
    hi, lo = jnp.concatenate(his, 1), jnp.concatenate(los, 1)
    both = jnp.concatenate([hi, lo], 0)
    out = lax.dot_general(hi, both, NT, preferred_element_type=F32)
    @pl.when(i == 0)
    def _(): acc[...] = out
    @pl.when(i > 0)
    def _(): acc[...] += out
    @pl.when(i == pl.num_programs(0) - 1)
    def _():
        b = acc[:, 128:]
        g_ref[...] = acc[:, :128] + b + b.T

def gram(h):
    past, rows, _ = h.shape
    return pl.pallas_call(
        gram_kernel, out_shape=jax.ShapeDtypeStruct((128, 128), F32), grid=(rows // 8,),
        in_specs=[pl.BlockSpec((past, 8, 128), lambda i: (0, i, 0))],
        out_specs=pl.BlockSpec((128, 128), lambda i: (0, 0)),
        scratch_shapes=[pltpu.VMEM((128, 256), F32)], name="gram")(h)

def basis_kernel(w_ref, h_ref, s_ref, o_ref):
    past = h_ref.shape[0]
    flat = h_ref.reshape(past * 8, 128)
    out = o_ref.reshape(128 * 8, 128)
    sf = s_ref.reshape(16, 128)
    whi, wlo = split(w_ref[...])
    lhs = jnp.concatenate([jnp.concatenate([whi, whi], 1), jnp.concatenate([wlo, wlo], 1)], 0)
    for j in range(0, 8, 2):
        ms = []
        for q in (j, j + 1):
            m = jnp.concatenate([flat[pl.ds(q, past, stride=8), :], sf[pl.ds(q, 2, stride=8), :]], axis=0)
            hi, lo = split(m)
            ms.append(jnp.concatenate([hi, lo], 0))
        r = jnp.dot(lhs, jnp.concatenate(ms, 1), preferred_element_type=F32)
        r = r[:128] + r[128:]
        out[pl.ds(j, 128, stride=8), :] = r[:, :128]
        out[pl.ds(j + 1, 128, stride=8), :] = r[:, 128:]

def basis(w, h, s):
    past, rows, _ = h.shape
    return pl.pallas_call(
        basis_kernel, out_shape=jax.ShapeDtypeStruct((128, rows, 128), F32), grid=(rows // 8,),
        in_specs=[pl.BlockSpec((128, 128), lambda i: (0, 0)), pl.BlockSpec((past, 8, 128), lambda i: (0, i, 0)),
                  pl.BlockSpec((2, 8, 128), lambda i: (0, i, 0))],
        out_specs=pl.BlockSpec((128, 8, 128), lambda i: (0, i, 0)), name="basis")(w, h, s)

def chol_kernel(g_ref, r_ref, w_ref, *, n):
    lane = lax.broadcasted_iota(jnp.int32, (8, 128), 1)
    sub = lax.broadcasted_iota(jnp.int32, (8, 128), 0)
    c = [g_ref[8 * b:8 * b + 8, :] for b in range(16)]
    for k in range(n):
        b0, s0 = k // 8, k % 8
        row = jnp.broadcast_to(c[b0][s0:s0 + 1, :], (8, 128))
        piv = jnp.broadcast_to(row[:, k:k + 1], (8, 128))
        inv = 1.0 / piv
        row = jnp.where(lane == k, 1.0, row) * inv
        for b in range(b0 if s0 < 7 else b0 + 1, 16):
            col = jnp.broadcast_to(c[b][:, k:k + 1], (8, 128))
            if b == b0:
                new = jnp.where(lane == k, 0.0, c[b]) - col * row
                c[b] = jnp.where(sub > s0, new, c[b])
            else:
                c[b] = jnp.where(lane == k, 0.0, c[b]) - col * row
    for b in range(16):
        rowi = sub + 8 * b
        d = jnp.sum(jnp.where(lane == rowi, c[b], 0.0), axis=1, keepdims=True)
        rs = 1.0 / jnp.sqrt(d)
        r_ref[8 * b:8 * b + 8, :] = jnp.where(lane >= rowi, c[b] * rs, 0.0)
        w_ref[8 * b:8 * b + 8, :] = jnp.where(lane < rowi, c[b] * rs, jnp.where(lane == rowi, rs, 0.0))

def chol(g):
    sh = jax.ShapeDtypeStruct((128, 128), F32)
    return pl.pallas_call(functools.partial(chol_kernel, n=128), out_shape=(sh, sh), name="chol")(g)

def lane_shift(x, left):
    n = x.shape[-1]
    lane = lax.broadcasted_iota(jnp.int32, x.shape, x.ndim - 1)
    if left:
        return jnp.where(lane == n - 1, 0.0, pltpu.roll(x, n - 1, x.ndim - 1))
    return jnp.where(lane == 0, 0.0, pltpu.roll(x, 1, x.ndim - 1))


def step_kernel(v_ref, k_ref, vxl, vxh, kxl, kxh, vyl, vyh, kyl, kyh, o_ref, s_ref, scr):
    nx, ny, nz = v_ref.shape
    chunk = 8

    def plane(x, vm_ref, km_ref, vp_ref, kp_ref):
        for y0 in range(0, ny, chunk):
            sl = slice(y0, y0 + chunk)
            v, k = v_ref[x, sl, :], k_ref[x, sl, :]
            acc = (k + kp_ref[sl, :]) * (vp_ref[sl, :] - v) + (k + km_ref[sl, :]) * (vm_ref[sl, :] - v)

            def up(ref, hi):
                if y0 + chunk < ny:
                    return ref[x, y0 + 1 : y0 + chunk + 1, :]
                return jnp.concatenate([ref[x, y0 + 1 : y0 + chunk, :], hi[0, pl.ds(x, 1), :]], 0)

            def down(ref, lo):
                if y0 > 0:
                    return ref[x, y0 - 1 : y0 + chunk - 1, :]
                return jnp.concatenate([lo[0, pl.ds(x, 1), :], ref[x, y0 : y0 + chunk - 1, :]], 0)

            acc += (k + up(k_ref, kyh)) * (up(v_ref, vyh) - v)
            acc += (k + down(k_ref, kyl)) * (down(v_ref, vyl) - v)
            acc += (k + lane_shift(k, True)) * (lane_shift(v, True) - v)
            acc += (k + lane_shift(k, False)) * (lane_shift(v, False) - v)
            o_ref[x, sl, :] = v + 0.5 * acc

    plane(0, vxl.at[0], kxl.at[0], v_ref.at[1], k_ref.at[1])

    def inner(x, carry):
        plane(x, v_ref.at[x - 1], k_ref.at[x - 1], v_ref.at[x + 1], k_ref.at[x + 1])
        return carry

    lax.fori_loop(1, nx - 1, inner, 0)
    plane(nx - 1, v_ref.at[nx - 2], k_ref.at[nx - 2], vxh.at[0], kxh.at[0])

    lane = lax.broadcasted_iota(jnp.int32, (8, 128), 1)

    def sampled(h, carry):
        out = jnp.zeros((8, 128), F32)
        for t in range(nz // 128):
            scr[ny * t : ny * (t + 1), :] = o_ref[2 * h, :, 128 * t : 128 * t + 128]
        for t in range(nz // 128):
            m = scr[pl.ds(ny * t, 8, stride=4), :]
            idx = 12 * lane - 128 * t
            ok = (idx >= 0) & (idx < 128)
            got = jnp.take_along_axis(m, jnp.where(ok, idx, 0), axis=1)
            out = jnp.where(ok, got, out)
        s_ref[h] = out
        return carry

    lax.fori_loop(0, nx // 2, sampled, 0)


def step(v, k, vx, kx, vy, ky):
    nx, ny, nz = v.shape
    spec = pl.BlockSpec((nx, ny, nz), lambda i: (0, 0, 0))
    xk = pl.BlockSpec((1, ny, nz), lambda i: (kx[0].shape[0] - 1, 0, 0))
    yk = pl.BlockSpec((1, nx, nz), lambda i: (ky[0].shape[0] - 1, 0, 0))
    xv = pl.BlockSpec((1, ny, nz), lambda i: (0, 0, 0))
    yv = pl.BlockSpec((1, nx, nz), lambda i: (0, 0, 0))
    return pl.pallas_call(
        step_kernel,
        out_shape=(
            jax.ShapeDtypeStruct(v.shape, F32),
            jax.ShapeDtypeStruct((nx // 2, ny // 4, nz // 12), F32),
        ),
        grid=(1,),
        in_specs=[spec, spec, xv, xv, xk, xk, yv, yv, yk, yk],
        out_specs=(spec, pl.BlockSpec((nx // 2, ny // 4, nz // 12), lambda i: (0, 0, 0))),
        scratch_shapes=[pltpu.VMEM((ny * nz // 128, 128), F32)],
        name="step",
    )(v, k, *vx, *kx, *vy, *ky)


def rows_kernel(h_ref, s1_ref, s2_ref, g_ref, o_ref, t_ref):
    i = pl.program_id(0)
    past = h_ref.shape[0]
    flat = h_ref.reshape(past * 8, 128)

    @pl.when(i == 0)
    def _():
        t_ref[...] = jnp.zeros_like(t_ref)

    t1, t2 = t_ref[0], t_ref[1]
    for j in range(8):
        a, b = s1_ref[0, j : j + 1, :], s2_ref[0, j : j + 1, :]
        m = jnp.concatenate([flat[pl.ds(j, past, stride=8), :], a, b], axis=0)
        t1 += m * a
        t2 += m * b
    t_ref[0], t_ref[1] = t1, t2

    @pl.when(i == pl.num_programs(0) - 1)
    def _():
        ones = jnp.ones((8, 128), F32)
        c1 = jnp.sum(t1, axis=1, keepdims=True)
        c2 = jnp.sum(t2, axis=1, keepdims=True)
        r1 = lax.dot_general(ones, t1, NT, precision=lax.Precision.HIGHEST, preferred_element_type=F32)
        r2 = lax.dot_general(ones, t2, NT, precision=lax.Precision.HIGHEST, preferred_element_type=F32)
        row = lax.broadcasted_iota(jnp.int32, (128, 128), 0)
        col = lax.broadcasted_iota(jnp.int32, (128, 128), 1)
        g = g_ref[...]
        g = jnp.where(col == past, c1, jnp.where(col == past + 1, c2, g))
        g = jnp.where(row == past, r1[:1], jnp.where(row == past + 1, r2[:1], g))
        o_ref[...] = g


def rows(h, s1, s2, g):
    past, n, _ = h.shape
    return pl.pallas_call(
        rows_kernel,
        out_shape=jax.ShapeDtypeStruct((128, 128), F32),
        grid=(n // 8,),
        in_specs=[
            pl.BlockSpec((past, 8, 128), lambda i: (0, i, 0)),
            pl.BlockSpec((1, 8, 128), lambda i: (i, 0, 0)),
            pl.BlockSpec((1, 8, 128), lambda i: (i, 0, 0)),
            pl.BlockSpec((128, 128), lambda i: (0, 0)),
        ],
        out_specs=pl.BlockSpec((128, 128), lambda i: (0, 0)),
        scratch_shapes=[pltpu.VMEM((2, 128, 128), F32)],
        name="rows",
    )(h, s1, s2, g)


def reversed_in(n, size, span):
    out = []
    for i in range(n):
        unit, rest = divmod(i, span)
        block, at = divmod(unit, size)
        out.append((i, (block * size + size - 1 - at) * span + rest))
    return out


def total(g):
    low = lax.axis_index("gy") % 2 == 0
    half = g.shape[0] // 2
    mine, other = jnp.where(low, g[:half], g[half:]), jnp.where(low, g[half:], g[:half])
    core = reversed_in(8, 2, 1)
    mine += lax.ppermute(other, "gy", core)
    for axis, n, span in (("gy", 8, 2), ("gx", 16, 1), ("gx", 16, 4)):
        for size in (2, 4):
            mine += lax.ppermute(mine, axis, reversed_in(n, size, span))
    other = lax.ppermute(mine, "gy", core)
    return jnp.where(low, jnp.concatenate([mine, other]), jnp.concatenate([other, mine]))


def beside(block, axis, dim):
    count = lax.axis_size(axis)
    forward = [(i, i + 1) for i in range(count - 1)]
    backward = [(b, a) for a, b in forward]
    size = block[0].shape[dim]

    def face(at):
        return jnp.stack([lax.index_in_dim(b, at, dim, keepdims=False) for b in block])

    return (
        lax.ppermute(face(size - 1), axis, forward),
        lax.ppermute(face(0), axis, backward),
    )


def body(field, kappa, history):
    past = history.shape[0]
    x = beside((field, kappa), "gx", 0)
    y = beside((field, kappa), "gy", 1)
    h = history.reshape(past, -1, 128)
    g = gram(h)
    first, s1 = step(field, kappa, x, x, y, y)
    second, s2 = step(first, kappa, beside((first,), "gx", 0), x, beside((first,), "gy", 1), y)
    g = rows(h, s1, s2, g)
    count = h.shape[1] * 128 * lax.axis_size("gx") * lax.axis_size("gy")
    factor, inverse = chol(total(g) / count)
    s = jnp.stack([s1, s2]).reshape(2, -1, 128)
    out = basis(inverse, h, s)
    return second, out.reshape((out.shape[0],) + history.shape[1:]), factor


def solution(mesh):
    return jax.shard_map(
        body,
        mesh=mesh,
        in_specs=(P("gx", "gy", None), P("gx", "gy", None), P(None, "gx", "gy", None)),
        out_specs=(P("gx", "gy", None), P(None, "gx", "gy", None), P()),
        check_vma=False,
    )
```

time: 419 us -> 141 us (0.34); the launches traced: 411 us -> 140 us
  waiting for transfers between devices: 153 us -> 15.6 us
  local copies, waits for them, and re-layouts: 123 us -> 11.9 us
  other arithmetic: 82.1 us -> 2.94 us
  Pallas kernels: 0 us -> 60.1 us
  starting transfers between devices: 24.2 us -> 49 us
  between operations: 14.5 us -> 0.86 us
  matrix products: 13.4 us -> 0 us
    psum x1 -> x0, waiting for transfers between devices: 135 us -> none  [body(): total = lax.psum(gram, ('gx', 'gy'))]
    reshape x2 -> x0, local copies, waits for them, and re-layouts: 77.3 us -> none  [sample(): return field.reshape(a // 2, 2, b // 4, 4, c // 12, 12)[:, 0, :, 0, :, 0]]
    pallas_call x0 -> x6, Pallas kernels: none -> 60.1 us  [the longest x2 20.7 us: step(): pl.pallas_call(step_kernel, out_shape=(jax.ShapeDtypeStruct(v.shape, F32)...]
    add x2 -> x7, other arithmetic: 41.3 us -> 0.82 us  [the longest x1 0.78 us: total(): mine += lax.ppermute(other, 'gy', core)]
    ppermute x8 -> x16, starting transfers between devices: 24.1 us -> 49 us  [the longest x6 20 us: total(): mine += lax.ppermute(mine, axis, reversed_in(n, size, span))]
    another operation x4 -> x5, other arithmetic: 22.2 us -> 0.71 us  [the longest x1 0.62 us: body(): s = jnp.stack([s1, s2]).reshape(2, -1, 128)]
    concatenate x4 -> x0, other arithmetic: 15.3 us -> none  [the longest x1 8.86 us: body(): jnp.concatenate([history, sample(first)[None], sample(second)[None]], 0)]
    unnamed x17 -> x20, local copies, waits for them, and re-layouts: 15.8 us -> 2.74 us
  transfers between devices with their start and end apart: 9 -> 16, of which waited for: 7 -> 10; matrix products, arithmetic and copies ran while one was open for 18% -> 3% of each run, Pallas kernels for 0% -> 5%
where the time goes in v1:
time: 141 us; the launch traced here: 140 us
  Pallas kernels  60.1 us (43%)
  starting transfers between devices  49 us (35%)
  waiting for transfers between devices  15.6 us (11%)
  local copies, waits for them, and re-layouts  11.9 us (8%)
  other arithmetic  2.94 us (2%)
    pallas_call x2, Pallas kernels, step(): pl.pallas_call(step_kernel, out_shape=(jax.ShapeDtypeStruct(v.shape, F32)...  20.7 us
    ppermute x6, starting transfers between devices, total(): mine += lax.ppermute(mine, axis, reversed_in(n, size, span))  20 us
    pallas_call x1, Pallas kernels, chol(): pl.pallas_call(functools.partial(chol_kernel, n=128), out_shape=(sh, sh),...  18.6 us
    ppermute x4, starting transfers between devices, beside(): lax.ppermute(face(size - 1), axis, forward)  16.4 us
    ppermute x6, waiting for transfers between devices, total(): mine += lax.ppermute(mine, axis, reversed_in(n, size, span))  8.92 us
    pallas_call x1, Pallas kernels, basis(): pl.pallas_call(basis_kernel, out_shape=jax.ShapeDtypeStruct((128, rows, 1...  7.83 us
    pallas_call x1, Pallas kernels, gram(): pl.pallas_call(gram_kernel, out_shape=jax.ShapeDtypeStruct((128, 128), F3...  6.75 us
    ppermute x4, starting transfers between devices, beside(): lax.ppermute(face(0), axis, backward)  6.43 us
  transfers between devices with their start and end apart: 16, of which 10 were waited for; matrix products, arithmetic and copies ran while one was open for 3% of the time, Pallas kernels for 5%

profile of v1, /device:TPU:1, one launch (start us, length us, event | category | flops | bytes accessed | tf_op | source)
XLA Modules:
  0.0 140.4 jit_solution(13068859192521124404)
XLA Ops:
  0.6 1.3 fusion.4
  2.0 1.3 collective-permute-start.1
  3.3 1.5 %fusion.2 = (f32[16,1,1536]{2,1,0:T(1,128)S(1)}, f32[16,1,1536]{2,1,0:T(1,128)S(1)}) fusion(f32[16,32,1536]{2,1,0:T(8,128)} %v_ref.1), kind=kLoop, calls=%fused_computation.16 | loop fusion | bytes 393216 | tf_op jit(solution)/shard_map/slice | solution.py:262
  4.8 1.5 %fusion.3 = (f32[16,1,1536]{2,1,0:T(1,128)S(1)}, f32[16,1,1536]{2,1,0:T(1,128)S(1)}) fusion(f32[16,32,1536]{2,1,0:T(8,128)} %k_ref.3), kind=kLoop, calls=%fused_computation.17 | loop fusion | bytes 393216 | tf_op jit(solution)/shard_map/slice | solution.py:262
  6.3 4.9 %collective-permute-start.2 = (f32[2,16,1536]{2,1,0:T(8,128)S(1)}, f32[2,16,1536]{2,1,0:T(8,128)S(1)}, u32[]{:S(2)}, u32[]{:S(2)}) collective-permute-start(f32[2,16,1536]{2,1,0:T(8,128)S(1)} %pad_maximum_fusion.2), channel_id=1, source_target_pairs={{0,1},{1,2},{2,3},{3,4},{4,5},{5,6},{6,7},{8,9},{9,10},{10,11},{11... | collective-permute-start | bytes 589832 | tf_op jit(solution)/shard_map/ppermute | solution.py:265
  11.3 4.3 %collective-permute-start = (f32[2,32,1536]{2,1,0:T(8,128)S(1)}, f32[2,32,1536]{2,1,0:T(8,128)S(1)}, u32[]{:S(2)}, u32[]{:S(2)}) collective-permute-start(f32[2,32,1536]{2,1,0:T(8,128)S(1)} %pad_maximum_fusion), channel_id=1, source_target_pairs={{0,8},{8,16},{16,24},{24,32},{32,40},{40,48},{48,56},{56,64},{64,7... | collective-permute-start | bytes 1179656 | tf_op jit(solution)/shard_map/ppermute | solution.py:265
  15.6 1.9 %collective-permute-start.3 = (f32[2,16,1536]{2,1,0:T(8,128)S(1)}, f32[2,16,1536]{2,1,0:T(8,128)S(1)}, u32[]{:S(2)}, u32[]{:S(2)}) collective-permute-start(f32[2,16,1536]{2,1,0:T(8,128)S(1)} %pad_maximum_fusion.3), channel_id=1, source_target_pairs={{1,0},{2,1},{3,2},{4,3},{5,4},{6,5},{7,6},{9,8},{10,9},{11,10},{12... | collective-permute-start | bytes 589832 | tf_op jit(solution)/shard_map/ppermute | solution.py:266
  17.6 5.0 %collective-permute-done.3.vyh.kyh = f32[2,16,1536]{2,1,0:T(8,128)S(1)} collective-permute-done((f32[2,16,1536]{2,1,0:T(8,128)S(1)}, f32[2,16,1536]{2,1,0:T(8,128)S(1)}, u32[]{:S(2)}, u32[]{:S(2)}) %collective-permute-start.3) | collective-permute-done | bytes 196640 | tf_op jit(solution)/shard_map/ppermute | solution.py:266
  22.6 0.0 collective-permute-done.1.vxh.kxh
  22.6 0.2 collective-permute-done.vxl.kxl
  22.8 0.5 copy-done.3
  23.3 0.1 copy-done
  23.5 0.7 copy-done.1
  24.2 10.3 %step.2 = (f32[16,32,1536]{2,1,0:T(8,128)}, f32[8,8,128]{2,1,0:T(8,128)}) custom-call(f32[16,32,1536]{2,1,0:T(8,128)} %v_ref.1, f32[16,32,1536]{2,1,0:T(8,128)} %k_ref.3, f32[2,32,1536]{2,1,0:T(8,128)} %copy-done.1, f32[2,32,1536]{2,1,0:T(8,128)} %copy-done, f32[2,32,1536]{2,1,0:T(8,128)} %copy-done.1, f32[2,32,1536]{2,1,0:T(8,128)} %copy-done, ...), custom_call_target="tpu_custom_call" | custom-call | tf_op jit(solution)/shard_map/step/pallas_call | solution.py:169
  34.5 3.7 %copy.10 = f32[16,32,1536]{2,0,1:T(8,128)S(1)} copy(f32[16,32,1536]{2,1,0:T(8,128)} %get-tuple-element.9.v_ref) | data formatting | bytes 6291456 | tf_op jit(solution)/shard_map/step/pallas_call | solution.py:169
  38.3 1.1 fusion.1
  39.3 3.2 %collective-permute-start.4 = (f32[1,32,1536]{2,1,0:T(8,128)S(1)}, f32[1,32,1536]{2,1,0:T(8,128)S(1)}, u32[]{:S(2)}, u32[]{:S(2)}) collective-permute-start(f32[1,32,1536]{2,1,0:T(8,128)S(1)} %get-tuple-element.18), channel_id=1, source_target_pairs={{0,8},{8,16},{16,24},{24,32},{32,40},{40,48},{48,56},{56,64},{64,7... | collective-permute-start | bytes 589832 | tf_op jit(solution)/shard_map/ppermute | solution.py:265
  42.5 1.3 collective-permute-start.5
  43.9 4.0 %collective-permute-start.6 = (f32[1,16,1536]{2,1,0:T(8,128)S(1)}, f32[1,16,1536]{2,1,0:T(8,128)S(1)}, u32[]{:S(2)}, u32[]{:S(2)}) collective-permute-start(f32[1,16,1536]{2,1,0:T(8,128)S(1)} %get-tuple-element.16), channel_id=1, source_target_pairs={{0,1},{1,2},{2,3},{3,4},{4,5},{5,6},{6,7},{8,9},{9,10},{10,11},{11... | collective-permute-start | bytes 294920 | tf_op jit(solution)/shard_map/ppermute | solution.py:265
  47.8 1.9 %collective-permute-start.7 = (f32[1,16,1536]{2,1,0:T(8,128)S(1)}, f32[1,16,1536]{2,1,0:T(8,128)S(1)}, u32[]{:S(2)}, u32[]{:S(2)}) collective-permute-start(f32[1,16,1536]{2,1,0:T(8,128)S(1)} %get-tuple-element.15), channel_id=1, source_target_pairs={{1,0},{2,1},{3,2},{4,3},{5,4},{6,5},{7,6},{9,8},{10,9},{11,10},{12... | collective-permute-start | bytes 294920 | tf_op jit(solution)/shard_map/ppermute | solution.py:266
  49.8 6.7 %gram.1.g_ref = f32[128,128]{1,0:T(8,128)} custom-call(f32[126,64,128]{2,1,0:T(8,128)} %bitcast.16), custom_call_target="tpu_custom_call" | custom-call | tf_op jit(solution)/shard_map/gram/pallas_call | solution.py:41
  56.6 0.6 copy-done.8
  57.1 0.1 copy-done.9
  57.2 0.1 copy-done.4
  57.3 0.7 copy-done.5
  57.9 10.4 %step.3 = (f32[16,32,1536]{2,1,0:T(8,128)}, f32[8,8,128]{2,1,0:T(8,128)}) custom-call(f32[16,32,1536]{2,1,0:T(8,128)} %get-tuple-element.9.v_ref, f32[16,32,1536]{2,1,0:T(8,128)} %k_ref.3, f32[1,32,1536]{2,1,0:T(8,128)} %copy-done.4, f32[1,32,1536]{2,1,0:T(8,128)} %copy-done.5, f32[2,32,1536]{2,1,0:T(8,128)} %copy-done.1, f32[2,32,1536]{2,1,0:T(8,128)} %copy-done, ...), custom_call_target="tpu_custom_call" | custom-call | tf_op jit(solution)/shard_map/step/pallas_call | solution.py:169
  68.3 6.2 %rows.1 = f32[128,128]{1,0:T(8,128)} custom-call(f32[126,64,128]{2,1,0:T(8,128)} %bitcast.17, f32[8,8,128]{2,1,0:T(8,128)} %get-tuple-element.11.s1_ref, f32[8,8,128]{2,1,0:T(8,128)} %get-tuple-element.12.s2_ref, f32[128,128]{1,0:T(8,128)} %gram.1.g_ref), custom_call_target="tpu_custom_call" | custom-call | tf_op jit(solution)/shard_map/rows/pallas_call | solution.py:217
  74.5 0.8 slice_select_fusion
  75.3 1.2 collective-permute-done.8
  76.5 0.8 select_add_fusion
  77.3 1.9 %collective-permute-start.9 = (f32[64,128]{1,0:T(8,128)S(1)}, f32[64,128]{1,0:T(8,128)S(1)}, u32[]{:S(2)}, u32[]{:S(2)}) collective-permute-start(f32[64,128]{1,0:T(8,128)S(1)} %select_add_fusion), channel_id=1, source_target_pairs={{0,2},{1,3},{2,0},{3,1},{4,6},{5,7},{6,4},{7,5},{8,10},{9,11},{10,... | collective-permute-start | bytes 98312 | tf_op jit(solution)/shard_map/ppermute | solution.py:250
  79.2 1.6 %collective-permute-done.9 = f32[64,128]{1,0:T(8,128)S(1)} collective-permute-done((f32[64,128]{1,0:T(8,128)S(1)}, f32[64,128]{1,0:T(8,128)S(1)}, u32[]{:S(2)}, u32[]{:S(2)}) %collective-permute-start.9) | collective-permute-done | bytes 32800 | tf_op jit(solution)/shard_map/ppermute | solution.py:250
  80.8 1.9 %collective-permute-start.10 = (f32[64,128]{1,0:T(8,128)S(1)}, f32[64,128]{1,0:T(8,128)S(1)}, u32[]{:S(2)}, u32[]{:S(2)}) collective-permute-start(f32[64,128]{1,0:T(8,128)S(1)} %add.27), channel_id=1, source_target_pairs={{0,6},{1,7},{2,4},{3,5},{4,2},{5,3},{6,0},{7,1},{8,14},{9,15},{10,... | collective-permute-start | bytes 98312 | tf_op jit(solution)/shard_map/ppermute | solution.py:250
  82.7 2.1 %collective-permute-done.10 = f32[64,128]{1,0:T(8,128)S(1)} collective-permute-done((f32[64,128]{1,0:T(8,128)S(1)}, f32[64,128]{1,0:T(8,128)S(1)}, u32[]{:S(2)}, u32[]{:S(2)}) %collective-permute-start.10) | collective-permute-done | bytes 32800 | tf_op jit(solution)/shard_map/ppermute | solution.py:250
  84.8 2.4 %collective-permute-start.11 = (f32[64,128]{1,0:T(8,128)S(1)}, f32[64,128]{1,0:T(8,128)S(1)}, u32[]{:S(2)}, u32[]{:S(2)}) collective-permute-start(f32[64,128]{1,0:T(8,128)S(1)} %add.28), channel_id=1, source_target_pairs={{0,8},{8,0},{16,24},{24,16},{32,40},{40,32},{48,56},{56,48},{64,72... | collective-permute-start | bytes 98312 | tf_op jit(solution)/shard_map/ppermute | solution.py:250
  87.1 1.3 collective-permute-done.11
  88.5 6.7 %collective-permute-start.12 = (f32[64,128]{1,0:T(8,128)S(1)}, f32[64,128]{1,0:T(8,128)S(1)}, u32[]{:S(2)}, u32[]{:S(2)}) collective-permute-start(f32[64,128]{1,0:T(8,128)S(1)} %add.29), channel_id=1, source_target_pairs={{0,24},{8,16},{16,8},{24,0},{32,56},{40,48},{48,40},{56,32},{64,88... | collective-permute-start | bytes 98312 | tf_op jit(solution)/shard_map/ppermute | solution.py:250
  95.1 1.3 collective-permute-done.12
  96.4 4.1 %collective-permute-start.13 = (f32[64,128]{1,0:T(8,128)S(1)}, f32[64,128]{1,0:T(8,128)S(1)}, u32[]{:S(2)}, u32[]{:S(2)}) collective-permute-start(f32[64,128]{1,0:T(8,128)S(1)} %add.30), channel_id=1, source_target_pairs={{0,32},{8,40},{16,48},{24,56},{32,0},{40,8},{48,16},{56,24},{64,96... | collective-permute-start | bytes 98312 | tf_op jit(solution)/shard_map/ppermute | solution.py:250
  100.6 1.3 collective-permute-done.13
  101.9 3.0 %collective-permute-start.14 = (f32[64,128]{1,0:T(8,128)S(1)}, f32[64,128]{1,0:T(8,128)S(1)}, u32[]{:S(2)}, u32[]{:S(2)}) collective-permute-start(f32[64,128]{1,0:T(8,128)S(1)} %add.31), channel_id=1, source_target_pairs={{0,96},{8,104},{16,112},{24,120},{32,64},{40,72},{48,80},{56,88},{... | collective-permute-start | bytes 98312 | tf_op jit(solution)/shard_map/ppermute | solution.py:250
  104.9 1.3 collective-permute-done.14
  106.2 6.2 %collective-permute-start.15 = (f32[64,128]{1,0:T(8,128)S(1)}, f32[64,128]{1,0:T(8,128)S(1)}, u32[]{:S(2)}, u32[]{:S(2)}) collective-permute-start(f32[64,128]{1,0:T(8,128)S(1)} %add.32), channel_id=1, source_target_pairs={{0,1},{1,0},{2,3},{3,2},{4,5},{5,4},{6,7},{7,6},{8,9},{9,8},{10,11... | collective-permute-start | bytes 98312 | tf_op jit(solution)/shard_map/ppermute | solution.py:251
  112.4 0.6 pad_maximum_fusion.4.s_ref
  113.0 0.2 collective-permute-done.15
  113.3 0.6 fusion.g_ref
  113.9 18.6 %chol.1 = (f32[128,128]{1,0:T(8,128)}, f32[128,128]{1,0:T(8,128)}) custom-call(f32[128,128]{1,0:T(8,128)} %fusion.g_ref), custom_call_target="tpu_custom_call" | custom-call | tf_op jit(solution)/shard_map/chol/pallas_call | solution.py:99
  132.6 7.8 %basis.1 = f32[128,64,128]{2,1,0:T(8,128)} custom-call(f32[128,128]{1,0:T(8,128)} %get-tuple-element.13.w_ref, f32[126,64,128]{2,1,0:T(8,128)} %bitcast.18, f32[2,64,128]{2,1,0:T(8,128)} %pad_maximum_fusion.4.s_ref), custom_call_target="tpu_custom_call" | custom-call | tf_op jit(solution)/shard_map/basis/pallas_call | solution.py:67
  (32 shorter events, 0.2 us)
Async XLA Ops:
  2.0 20.7 %collective-permute-start.1 = (f32[2,32,1536]{2,1,0:T(8,128)S(1)}, f32[2,32,1536]{2,1,0:T(8,128)S(1)}, u32[]{:S(2)}, u32[]{:S(2)}) collective-permute-start(f32[2,32,1536]{2,1,0:T(8,128)S(1)} %pad_maximum_fusion.1), channel_id=1, source_target_pairs={{8,0},{16,8},{24,16},{32,24},{40,32},{48,40},{56,48},{64,56},{72,6... | collective-permute-start | bytes 1179656 | tf_op jit(solution)/shard_map/ppermute | solution.py:266
  6.3 11.2 %collective-permute-start.2 = (f32[2,16,1536]{2,1,0:T(8,128)S(1)}, f32[2,16,1536]{2,1,0:T(8,128)S(1)}, u32[]{:S(2)}, u32[]{:S(2)}) collective-permute-start(f32[2,16,1536]{2,1,0:T(8,128)S(1)} %pad_maximum_fusion.2), channel_id=1, source_target_pairs={{0,1},{1,2},{2,3},{3,4},{4,5},{5,6},{6,7},{8,9},{9,10},{10,11},{11... | collective-permute-start | bytes 589832 | tf_op jit(solution)/shard_map/ppermute | solution.py:265
  11.3 11.5 %collective-permute-start = (f32[2,32,1536]{2,1,0:T(8,128)S(1)}, f32[2,32,1536]{2,1,0:T(8,128)S(1)}, u32[]{:S(2)}, u32[]{:S(2)}) collective-permute-start(f32[2,32,1536]{2,1,0:T(8,128)S(1)} %pad_maximum_fusion), channel_id=1, source_target_pairs={{0,8},{8,16},{16,24},{24,32},{32,40},{40,48},{48,56},{56,64},{64,7... | collective-permute-start | bytes 1179656 | tf_op jit(solution)/shard_map/ppermute | solution.py:265
  15.6 7.0 %collective-permute-start.3 = (f32[2,16,1536]{2,1,0:T(8,128)S(1)}, f32[2,16,1536]{2,1,0:T(8,128)S(1)}, u32[]{:S(2)}, u32[]{:S(2)}) collective-permute-start(f32[2,16,1536]{2,1,0:T(8,128)S(1)} %pad_maximum_fusion.3), channel_id=1, source_target_pairs={{1,0},{2,1},{3,2},{4,3},{5,4},{6,5},{7,6},{9,8},{10,9},{11,10},{12... | collective-permute-start | bytes 589832 | tf_op jit(solution)/shard_map/ppermute | solution.py:266
  17.6 5.3 %copy-start.2 = (f32[2,16,1536]{2,1,0:T(8,128)}, f32[2,16,1536]{2,1,0:T(8,128)S(1)}, u32[]{:S(2)}) copy-start(f32[2,16,1536]{2,1,0:T(8,128)S(1)} %collective-permute-done.2.vyl.kyl) | copy-start | bytes 589828
  22.6 0.7 copy-start.3
  22.6 0.8 copy-start
  23.4 0.7 copy-start.1
  39.3 17.2 %collective-permute-start.4 = (f32[1,32,1536]{2,1,0:T(8,128)S(1)}, f32[1,32,1536]{2,1,0:T(8,128)S(1)}, u32[]{:S(2)}, u32[]{:S(2)}) collective-permute-start(f32[1,32,1536]{2,1,0:T(8,128)S(1)} %get-tuple-element.18), channel_id=1, source_target_pairs={{0,8},{8,16},{16,24},{24,32},{32,40},{40,48},{48,56},{56,64},{64,7... | collective-permute-start | bytes 589832 | tf_op jit(solution)/shard_map/ppermute | solution.py:265
  42.5 14.0 %collective-permute-start.5 = (f32[1,32,1536]{2,1,0:T(8,128)S(1)}, f32[1,32,1536]{2,1,0:T(8,128)S(1)}, u32[]{:S(2)}, u32[]{:S(2)}) collective-permute-start(f32[1,32,1536]{2,1,0:T(8,128)S(1)} %get-tuple-element.17), channel_id=1, source_target_pairs={{8,0},{16,8},{24,16},{32,24},{40,32},{48,40},{56,48},{64,56},{72,6... | collective-permute-start | bytes 589832 | tf_op jit(solution)/shard_map/ppermute | solution.py:266
  43.9 12.7 %collective-permute-start.6 = (f32[1,16,1536]{2,1,0:T(8,128)S(1)}, f32[1,16,1536]{2,1,0:T(8,128)S(1)}, u32[]{:S(2)}, u32[]{:S(2)}) collective-permute-start(f32[1,16,1536]{2,1,0:T(8,128)S(1)} %get-tuple-element.16), channel_id=1, source_target_pairs={{0,1},{1,2},{2,3},{3,4},{4,5},{5,6},{6,7},{8,9},{9,10},{10,11},{11... | collective-permute-start | bytes 294920 | tf_op jit(solution)/shard_map/ppermute | solution.py:265
  47.8 8.7 %collective-permute-start.7 = (f32[1,16,1536]{2,1,0:T(8,128)S(1)}, f32[1,16,1536]{2,1,0:T(8,128)S(1)}, u32[]{:S(2)}, u32[]{:S(2)}) collective-permute-start(f32[1,16,1536]{2,1,0:T(8,128)S(1)} %get-tuple-element.15), channel_id=1, source_target_pairs={{1,0},{2,1},{3,2},{4,3},{5,4},{6,5},{7,6},{9,8},{10,9},{11,10},{12... | collective-permute-start | bytes 294920 | tf_op jit(solution)/shard_map/ppermute | solution.py:266
  56.5 0.6 copy-start.8
  56.5 0.7 copy-start.9
  56.5 0.7 copy-start.4
  57.3 0.7 copy-start.5
  68.3 44.1 %copy-start.6 = (f32[8,8,128]{2,1,0:T(8,128)S(1)}, f32[8,8,128]{2,1,0:T(8,128)}, u32[]{:S(2)}) copy-start(f32[8,8,128]{2,1,0:T(8,128)} %get-tuple-element.11.s1_ref) | copy-start | bytes 98308
  68.3 44.1 %copy-start.7 = (f32[8,8,128]{2,1,0:T(8,128)S(1)}, f32[8,8,128]{2,1,0:T(8,128)}, u32[]{:S(2)}) copy-start(f32[8,8,128]{2,1,0:T(8,128)} %get-tuple-element.12.s2_ref) | copy-start | bytes 98308
  75.3 1.2 collective-permute-start.8
  77.3 3.5 %collective-permute-start.9 = (f32[64,128]{1,0:T(8,128)S(1)}, f32[64,128]{1,0:T(8,128)S(1)}, u32[]{:S(2)}, u32[]{:S(2)}) collective-permute-start(f32[64,128]{1,0:T(8,128)S(1)} %select_add_fusion), channel_id=1, source_target_pairs={{0,2},{1,3},{2,0},{3,1},{4,6},{5,7},{6,4},{7,5},{8,10},{9,11},{10,... | collective-permute-start | bytes 98312 | tf_op jit(solution)/shard_map/ppermute | solution.py:250
  80.8 4.0 %collective-permute-start.10 = (f32[64,128]{1,0:T(8,128)S(1)}, f32[64,128]{1,0:T(8,128)S(1)}, u32[]{:S(2)}, u32[]{:S(2)}) collective-permute-start(f32[64,128]{1,0:T(8,128)S(1)} %add.27), channel_id=1, source_target_pairs={{0,6},{1,7},{2,4},{3,5},{4,2},{5,3},{6,0},{7,1},{8,14},{9,15},{10,... | collective-permute-start | bytes 98312 | tf_op jit(solution)/shard_map/ppermute | solution.py:250
  84.8 3.7 %collective-permute-start.11 = (f32[64,128]{1,0:T(8,128)S(1)}, f32[64,128]{1,0:T(8,128)S(1)}, u32[]{:S(2)}, u32[]{:S(2)}) collective-permute-start(f32[64,128]{1,0:T(8,128)S(1)} %add.28), channel_id=1, source_target_pairs={{0,8},{8,0},{16,24},{24,16},{32,40},{40,32},{48,56},{56,48},{64,72... | collective-permute-start | bytes 98312 | tf_op jit(solution)/shard_map/ppermute | solution.py:250
  88.5 8.0 %collective-permute-start.12 = (f32[64,128]{1,0:T(8,128)S(1)}, f32[64,128]{1,0:T(8,128)S(1)}, u32[]{:S(2)}, u32[]{:S(2)}) collective-permute-start(f32[64,128]{1,0:T(8,128)S(1)} %add.29), channel_id=1, source_target_pairs={{0,24},{8,16},{16,8},{24,0},{32,56},{40,48},{48,40},{56,32},{64,88... | collective-permute-start | bytes 98312 | tf_op jit(solution)/shard_map/ppermute | solution.py:250
  96.4 5.4 %collective-permute-start.13 = (f32[64,128]{1,0:T(8,128)S(1)}, f32[64,128]{1,0:T(8,128)S(1)}, u32[]{:S(2)}, u32[]{:S(2)}) collective-permute-start(f32[64,128]{1,0:T(8,128)S(1)} %add.30), channel_id=1, source_target_pairs={{0,32},{8,40},{16,48},{24,56},{32,0},{40,8},{48,16},{56,24},{64,96... | collective-permute-start | bytes 98312 | tf_op jit(solution)/shard_map/ppermute | solution.py:250
  101.9 4.3 %collective-permute-start.14 = (f32[64,128]{1,0:T(8,128)S(1)}, f32[64,128]{1,0:T(8,128)S(1)}, u32[]{:S(2)}, u32[]{:S(2)}) collective-permute-start(f32[64,128]{1,0:T(8,128)S(1)} %add.31), channel_id=1, source_target_pairs={{0,96},{8,104},{16,112},{24,120},{32,64},{40,72},{48,80},{56,88},{... | collective-permute-start | bytes 98312 | tf_op jit(solution)/shard_map/ppermute | solution.py:250
  106.2 7.1 %collective-permute-start.15 = (f32[64,128]{1,0:T(8,128)S(1)}, f32[64,128]{1,0:T(8,128)S(1)}, u32[]{:S(2)}, u32[]{:S(2)}) collective-permute-start(f32[64,128]{1,0:T(8,128)S(1)} %add.32), channel_id=1, source_target_pairs={{0,1},{1,0},{2,3},{3,2},{4,5},{5,4},{6,7},{7,6},{8,9},{9,8},{10,11... | collective-permute-start | bytes 98312 | tf_op jit(solution)/shard_map/ppermute | solution.py:251
